TPU v7x, 512 devices: a whole 4x8x8 slice. The times are simulated.
512 devices in a mesh: grp: 64 (over y, z), tp: 8 (over x, core).
Axes of the slice: x: 4, y: 8, z: 8, core: 2. Of those that a mesh axis runs over, the one named last changes fastest.
Arguments:
- queries: bfloat16 [512, 2048], P('grp', 'tp'), may hold values from -8 to 8
- new_kv: bfloat16 [512, 2, 512], P('grp', None, 'tp'), may hold values from -6 to 6
- home_cache: bfloat16 [512, 2, 8, 512, 128], P('grp', None, 'tp'), may hold values from -28 to 28
- help_cache: bfloat16 [256, 2, 8, 512, 128], P('grp', None, 'tp'), may hold values from -6 to 6
- lengths: int32 [512], P('grp'), may hold values from 2 to 2048, as said below
- split_at: int32 [512], P('grp'), may hold values from 1 to 1024, as said below
- helper_req: int32 [256], P('grp'), may hold values from 0 to 511, as said below
- out_weight: bfloat16 [2048, 2048], P('tp'), may hold values from -0.125 to 0.125
Outputs:
- attn_out: bfloat16 [512, 2048], P('grp', 'tp')
Inputs may be any that keep to these rules, and one draw needn't show every extreme that they name: `lengths`: in each aligned block of 8 requests exactly 4 have more than 1024 cached positions. `split_at`: equal to the length for requests of 1024 positions or fewer; otherwise between length - 1024 and min(1024, length - 1). `helper_req`: groups come in pairs; the 4 helper slots of a group serve, in increasing order, the requests of its partner group that have more than 1024 positions, so each such request has exactly one helper slot and all values are distinct.
All inputs are finite; a program needn't handle non-finite values.
Results may differ from a plain program's by a relative error of at most 0.007.
Values may be sent and summed in bfloat16 or wider, within the bound.
A program may use at most 192 MiB of HBM per device.

v0:
```python
import jax
import jax.numpy as jnp
from jax import lax
from jax.sharding import PartitionSpec as P


def attend(queries, cache, count, fresh):
    row_count = queries.shape[0]
    kv_heads = cache.shape[2]
    head_width = cache.shape[4] // 2
    context = cache.shape[3] * 2
    group_size = queries.shape[1] // (kv_heads * head_width)
    score_scale = head_width ** (-0.5)
    head_rows = queries.reshape(row_count, kv_heads, group_size, head_width)
    key_rows = cache[:, 0].reshape(row_count, kv_heads, context, head_width)
    value_rows = cache[:, 1].reshape(row_count, kv_heads, context, head_width)
    scores = (
        jnp.einsum("nkgd,nkpd->nkgp", head_rows, key_rows, preferred_element_type=jnp.float32)
        * score_scale
    )
    inside = (jnp.arange(context)[None, :] < count[:, None])[:, None, None, :]
    top_score = jnp.max(jnp.where(inside, scores, -1e30), axis=-1)
    if fresh is not None:
        fresh_key = fresh[:, 0].reshape(row_count, kv_heads, head_width)
        fresh_score = (
            jnp.einsum("nkgd,nkd->nkg", head_rows, fresh_key, preferred_element_type=jnp.float32)
            * score_scale
        )
        top_score = jnp.maximum(top_score, fresh_score)
    weights = jnp.where(inside, jnp.exp(scores - top_score[..., None]), 0.0).astype(jnp.bfloat16)
    weight_sum = jnp.sum(weights.astype(jnp.float32), axis=-1)
    mixed_sum = jnp.einsum(
        "nkgp,nkpd->nkgd", weights, value_rows, preferred_element_type=jnp.float32
    )
    if fresh is not None:
        fresh_weight = lax.optimization_barrier(
            jnp.exp(fresh_score - top_score).astype(jnp.bfloat16)
        ).astype(jnp.float32)
        weight_sum = weight_sum + fresh_weight
        fresh_value = fresh[:, 1].reshape(row_count, kv_heads, 1, head_width).astype(jnp.float32)
        mixed_sum = mixed_sum + fresh_weight[..., None] * fresh_value
    return (
        top_score.reshape(row_count, -1),
        weight_sum.reshape(row_count, -1),
        mixed_sum.reshape(row_count, -1, head_width),
    )


def per_device(queries, new_kv, home_cache, help_cache, lengths, split_at, helper_req, out_weight):
    row_count = queries.shape[0]
    total_rows = row_count * lax.axis_size("grp")
    row_ids = jnp.arange(total_rows)
    help_sel = helper_req[:, None] == row_ids[None, :]
    everyone, all_lengths, all_splits = (
        lax.all_gather(queries, "grp", axis=0, tiled=True),
        lax.all_gather(lengths, "grp", axis=0, tiled=True),
        lax.all_gather(split_at, "grp", axis=0, tiled=True),
    )
    help_queries = jnp.dot(
        help_sel.astype(jnp.bfloat16), everyone, preferred_element_type=jnp.float32
    ).astype(jnp.bfloat16)
    help_count = jnp.sum(jnp.where(help_sel, (all_lengths - all_splits)[None, :], 0), axis=1)
    home_m, home_l, home_u = attend(queries, home_cache, split_at, new_kv)
    help_m, help_l, help_u = attend(help_queries, help_cache, help_count, None)
    row_start = lax.axis_index("grp") * row_count
    all_m, all_l, all_u, all_req = (
        lax.all_gather(help_m, "grp", axis=0, tiled=True),
        lax.all_gather(help_l, "grp", axis=0, tiled=True),
        lax.all_gather(help_u, "grp", axis=0, tiled=True),
        lax.all_gather(helper_req, "grp", axis=0, tiled=True),
    )
    own_ids = row_start + jnp.arange(row_count)
    own_sel = own_ids[:, None] == all_req[None, :]
    far_m = jnp.max(jnp.where(own_sel[:, :, None], all_m[None], -1e30), axis=1)
    far_l = jnp.sum(jnp.where(own_sel[:, :, None], all_l[None], 0.0), axis=1)
    far_u = jnp.sum(jnp.where(own_sel[:, :, None, None], all_u[None], 0.0), axis=1)
    top_score = jnp.maximum(home_m, far_m)
    home_e = jnp.exp(home_m - top_score)
    far_e = jnp.exp(far_m - top_score)
    numerator = home_u * home_e[..., None] + far_u * far_e[..., None]
    denominator = home_l * home_e + far_l * far_e
    heads_out = numerator / denominator[..., None]
    mix = heads_out.reshape(row_count, -1).astype(jnp.bfloat16)
    partial_out = jnp.dot(mix, out_weight, preferred_element_type=jnp.float32)
    return lax.psum_scatter(partial_out, "tp", scatter_dimension=1, tiled=True).astype(jnp.bfloat16)


def solution(mesh):
    return jax.shard_map(
        per_device,
        mesh=mesh,
        in_specs=(
            P("grp", "tp"),
            P("grp", None, "tp"),
            P("grp", None, "tp", None, None),
            P("grp", None, "tp", None, None),
            P("grp"),
            P("grp"),
            P("grp"),
            P("tp", None),
        ),
        out_specs=P("grp", "tp"),
        check_vma=False,
    )
```

profile of v0, /device:TPU:8, one launch (start us, length us, event | category | flops | bytes accessed | tf_op | source)
XLA Modules:
  0.0 292.7 jit_solution(9021844830264315112)
XLA Ops:
  6.5 0.0 reduce-scatter.2.cloned.1.call-start
  6.5 0.9 reshape.232
  7.4 55.8 %all_gather.24 = bf16[512,256]{1,0:T(8,128)(2,1)S(1)} all-gather(bf16[8,256]{1,0:T(8,128)(2,1)} %param.8), channel_id=1, replica_groups=mesh['grp'=64,'tp'=8] {'grp'}, dimensions={0}, use_global_device_ids=true | all-gather | bytes 266240 | tf_op jit(solution)/shard_map/all_gather | solution.py:55
  63.2 1.3 dynamic-slice
  65.7 0.7 iota_compare_fusion
  66.5 0.8 dynamic-update-slice.2
  67.3 0.8 dynamic-update-slice.1
  68.1 0.8 dynamic-update-slice
  69.0 22.3 %all-reduce.3 = (s32[512]{0:T(512)S(1)}, s32[512]{0:T(512)S(1)}, s32[256]{0:T(256)S(1)}) all-reduce(s32[512]{0:T(512)S(1)} %dynamic-update-slice.1, s32[512]{0:T(512)S(1)} %dynamic-update-slice.2, s32[256]{0:T(256)S(1)} %dynamic-update-slice), channel_id=1, replica_groups=mesh['grp'=64,'tp'=8] {'grp'}, use_global_device_ids=true, to_apply=%add.1 | all-reduce | flops 1280 | bytes 10240
  91.3 0.8 select_reduce_fusion.5
  92.1 0.1 iota_compare_fusion.1
  92.2 0.8 slice_convert_fusion
  93.0 0.8 convolution_convert_fusion
  93.8 0.1 reshape.236
  93.9 1.3 fusion.14
  95.2 0.4 reshape.237
  95.6 0.5 select_reduce_fusion.2
  96.1 0.2 convert_reduce_fusion.1
  96.2 46.9 %all-gather.1 = f32[64,4,4]{2,1,0:T(4,128)S(1)} all-gather(f32[1,4,4]{2,1,0:T(4,128)S(1)} %bitcast.43), channel_id=1, replica_groups=mesh['grp'=64,'tp'=8] {'grp'}, dimensions={0}, use_global_device_ids=true | all-gather | bytes 4160 | tf_op jit(solution)/shard_map/all_gather | solution.py:68
  143.2 0.1 copy.46
  143.2 47.7 %all-gather = f32[64,4,4]{2,1,0:T(4,128)S(1)} all-gather(f32[1,4,4]{2,1,0:T(4,128)S(1)} %bitcast.40), channel_id=1, replica_groups=mesh['grp'=64,'tp'=8] {'grp'}, dimensions={0}, use_global_device_ids=true | all-gather | bytes 4160 | tf_op jit(solution)/shard_map/all_gather | solution.py:67
  190.9 0.1 copy.39
  191.0 0.1 broadcast_compare_fusion
  191.1 0.1 select_reduce_fusion.4
  191.2 0.1 copy.40
  191.3 0.1 copy.47
  191.4 0.4 reshape.238
  191.8 0.3 fusion.10
  192.1 47.3 %all_gather.26 = f32[256,4,64]{2,1,0:T(4,128)S(1)} all-gather(f32[4,4,64]{2,1,0:T(4,128)S(1)} %fusion.10), channel_id=1, replica_groups=mesh['grp'=64,'tp'=8] {'grp'}, dimensions={0}, use_global_device_ids=true | all-gather | bytes 266240 | tf_op jit(solution)/shard_map/all_gather | solution.py:69
  239.4 0.2 copy.42
  239.6 0.4 select_reduce_fusion
  240.0 3.1 %fusion.13 = (bf16[8,1,1,512,128]{4,3,2,1,0:T(8,128)(2,1)}, bf16[8,1,1,512,128]{4,3,2,1,0:T(8,128)(2,1)}) fusion(bf16[8,2,1,512,128]{4,3,2,1,0:T(8,128)(2,1)} %param.10), kind=kLoop, calls=%fused_computation.39 | loop fusion | bytes 4194304 | tf_op jit(solution)/shard_map/slice | solution.py:15
  243.1 2.7 reshape.233
  245.8 0.1 fusion.7
  245.9 0.7 select_reduce_fusion.1
  246.7 0.1 copy.36
  246.8 0.1 copy.37
  246.9 0.2 convert_reduce_fusion
  247.1 0.1 copy.44
  247.2 0.1 copy.45
  247.3 2.7 reshape.235
  250.1 0.4 fusion.3
  250.5 0.1 convert_element_type.60
  250.6 0.0 copy-done
  250.6 0.9 fusion.15
  251.5 0.0 reduce-scatter.2.cloned.1.call-update
  251.5 33.1 %reduce-scatter.2.cloned.1.call-done = f32[8,256]{1,0:T(8,128)} async-done(((f32[8,2048]{1,0:T(8,128)}), f32[8,256]{1,0:T(8,128)}) %reduce-scatter.2.cloned.1.call-update) | async-done | bytes 8208 | tf_op jit(solution)/shard_map/reduce_scatter | solution.py:85
  284.6 1.3 convert_element_type.61
  (11 shorter events, 0.1 us)
Async XLA Ops:
  6.5 244.1 %copy-start = (bf16[256,2048]{1,0:T(8,128)(2,1)S(1)}, bf16[256,2048]{1,0:T(8,128)(2,1)}, u32[]{:S(2)}) copy-start(bf16[256,2048]{1,0:T(8,128)(2,1)} %param.15) | copy-start | bytes 3145732
  6.5 278.0 %reduce-scatter.2.cloned.1.call-start = ((), (), s32[]{:S(2)}) async-start(), calls=%async_computation.1 | async-start | bytes 73728 | tf_op jit(solution)/shard_map/reduce_scatter | solution.py:85
Sparse Core Ops, SparseCore 0:
  251.6 32.9 reduce-scatter.1
where the time goes:
time: 293 us
  blocking collectives  220 us (75%)
  waiting for transfers between devices  33.1 us (11%)
  local copies, waits for them, and re-layouts  16.4 us (6%)
  between operations  14.8 us (5%)
  other arithmetic  4.71 us (2%)
  matrix products  3.79 us (1%)
    all_gather x1, blocking collectives, per_device(): lax.all_gather(queries, 'grp', axis=0, tiled=True)  55.8 us
    all_gather x1, blocking collectives, per_device(): lax.all_gather(help_m, 'grp', axis=0, tiled=True)  47.7 us
    all_gather x1, blocking collectives, per_device(): lax.all_gather(help_u, 'grp', axis=0, tiled=True)  47.3 us
    all_gather x1, blocking collectives, per_device(): lax.all_gather(help_l, 'grp', axis=0, tiled=True)  46.9 us
    reduce_scatter x1, waiting for transfers between devices, per_device(): lax.psum_scatter(partial_out, 'tp', scatter_dimension=1, tiled=True)  33.1 us
    unnamed x1, blocking collectives  22.3 us
    another operation x6, local copies, waits for them, and re-layouts  7.24 us
  transfers between devices with their start and end apart: 1, of which 1 were waited for; matrix products, arithmetic and copies ran while one was open for 0% of the time, Pallas kernels for 0%

commit v1 on v0

--- a/solution.py
+++ b/solution.py
@@ -47,6 +47,15 @@
 
 
 def per_device(queries, new_kv, home_cache, help_cache, lengths, split_at, helper_req, out_weight):
+
+    def _carry_entries(xin):
+        return jnp.concatenate(
+            lax.all_to_all(
+                jnp.stack([xin for _ in range(lax.axis_size("grp"))], axis=0), "grp", 0, 0
+            ),
+            axis=0,
+        )
+
     row_count = queries.shape[0]
     total_rows = row_count * lax.axis_size("grp")
     row_ids = jnp.arange(total_rows)
@@ -66,7 +75,7 @@
     all_m, all_l, all_u, all_req = (
         lax.all_gather(help_m, "grp", axis=0, tiled=True),
         lax.all_gather(help_l, "grp", axis=0, tiled=True),
-        lax.all_gather(help_u, "grp", axis=0, tiled=True),
+        _carry_entries(help_u),
         lax.all_gather(helper_req, "grp", axis=0, tiled=True),
     )
     own_ids = row_start + jnp.arange(row_count)

time: 293 us -> 271 us (0.925)
  blocking collectives: 220 us -> 175 us
  local copies, waits for them, and re-layouts: 16.4 us -> 26.8 us
  starting transfers between devices: 0.01 us -> 8.33 us
    all_gather x1 -> x0, blocking collectives: 47.3 us -> none  [per_device(): lax.all_gather(help_u, 'grp', axis=0, tiled=True)]
    unnamed x1, blocking collectives: 22.3 us -> 31.1 us
    all_gather x1, blocking collectives: 55.8 us -> 47 us  [per_device(): lax.all_gather(queries, 'grp', axis=0, tiled=True)]
    all_to_all x0 -> x1, starting transfers between devices: none -> 8.29 us  [_carry_entries(): lax.all_to_all(jnp.stack([xin for _ in range(lax.axis_size('grp'))], axis...]
    unnamed x12 -> x27, local copies, waits for them, and re-layouts: 3.95 us -> 7.2 us
  transfers between devices with their start and end apart: 1 -> 2, of which waited for: 1 -> 1; matrix products, arithmetic and copies ran while one was open for 0% -> 6% of each run, Pallas kernels for 0% -> 0%
where the time goes in v1:
time: 271 us
  blocking collectives  175 us (65%)
  waiting for transfers between devices  34.4 us (13%)
  local copies, waits for them, and re-layouts  26.8 us (10%)
  between operations  14.9 us (5%)
  starting transfers between devices  8.33 us (3%)
  other arithmetic  7.35 us (3%)
  matrix products  4.5 us (2%)
    all_gather x1, blocking collectives, per_device(): lax.all_gather(help_l, 'grp', axis=0, tiled=True)  49 us
    all_gather x1, blocking collectives, per_device(): lax.all_gather(help_m, 'grp', axis=0, tiled=True)  47.4 us
    all_gather x1, blocking collectives, per_device(): lax.all_gather(queries, 'grp', axis=0, tiled=True)  47 us
    reduce_scatter x1, waiting for transfers between devices, per_device(): lax.psum_scatter(partial_out, 'tp', scatter_dimension=1, tiled=True)  34.4 us
    unnamed x1, blocking collectives  31.1 us
    all_to_all x1, starting transfers between devices, _carry_entries(): lax.all_to_all(jnp.stack([xin for _ in range(lax.axis_size('grp'))], axis...  8.29 us
    another operation x6, local copies, waits for them, and re-layouts  7.7 us
    unnamed x27, local copies, waits for them, and re-layouts  7.2 us
  transfers between devices with their start and end apart: 2, of which 1 were waited for; matrix products, arithmetic and copies ran while one was open for 6% of the time, Pallas kernels for 0%

profile of v1, /device:TPU:8, one launch (start us, length us, event | category | flops | bytes accessed | tf_op | source)
XLA Modules:
  0.0 270.7 jit_solution(14226487510436149355)
XLA Ops:
  6.5 1.4 dynamic-slice
  9.2 0.9 dynamic-update-slice.1
  10.1 0.8 dynamic-update-slice.2
  10.9 0.8 dynamic-update-slice
  11.7 31.1 %all-reduce.3 = (s32[512]{0:T(512)S(1)}, s32[512]{0:T(512)S(1)}, s32[256]{0:T(256)S(1)}) all-reduce(s32[512]{0:T(512)S(1)} %dynamic-update-slice.1, s32[512]{0:T(512)S(1)} %dynamic-update-slice.2, s32[256]{0:T(256)S(1)} %dynamic-update-slice), channel_id=1, replica_groups=mesh['grp'=64,'tp'=8] {'grp'}, use_global_device_ids=true, to_apply=%add.1 | all-reduce | flops 1280 | bytes 10240
  42.8 0.8 select_reduce_fusion.5
  43.7 47.0 %all_gather.21 = bf16[512,256]{1,0:T(8,128)(2,1)S(1)} all-gather(bf16[8,256]{1,0:T(8,128)(2,1)} %param.8), channel_id=1, replica_groups=mesh['grp'=64,'tp'=8] {'grp'}, dimensions={0}, use_global_device_ids=true | all-gather | bytes 266240 | tf_op jit(solution)/shard_map/all_gather | solution.py:64
  90.7 0.8 convolution_convert_fusion
  91.5 0.1 reshape.237
  91.6 2.1 fusion.14
  93.7 0.4 reshape.238
  94.1 1.6 reshape.239
  95.8 0.5 select_reduce_fusion.2
  96.3 0.3 fusion.10
  96.6 0.1 broadcast_bitcast_fusion
  96.7 1.2 reshape.263
  97.9 8.3 %all-to-all-start = ((f32[64,1,1024]{2,1,0:T(1,128)}), f32[64,1,1024]{2,1,0:T(1,128)S(1)}, u32[]{:S(2)}, u32[]{:S(2)}) async-start(f32[64,1,1024]{2,1,0:T(1,128)} %reshape.263), calls=%async_computation | async-start | bytes 524288 | tf_op jit(solution)/shard_map/all_to_all | solution.py:53
  106.3 0.1 reshape.233
  106.4 0.2 convert_reduce_fusion.1
  106.6 0.6 slice_convert_fusion
  107.2 49.0 %all-gather.1 = f32[64,4,4]{2,1,0:T(4,128)S(1)} all-gather(f32[1,4,4]{2,1,0:T(4,128)S(1)} %bitcast.49), channel_id=1, replica_groups=mesh['grp'=64,'tp'=8] {'grp'}, dimensions={0}, use_global_device_ids=true | all-gather | bytes 4160 | tf_op jit(solution)/shard_map/all_gather | solution.py:77
  156.3 47.4 %all-gather = f32[64,4,4]{2,1,0:T(4,128)S(1)} all-gather(f32[1,4,4]{2,1,0:T(4,128)S(1)} %bitcast.46), channel_id=1, replica_groups=mesh['grp'=64,'tp'=8] {'grp'}, dimensions={0}, use_global_device_ids=true | all-gather | bytes 4160 | tf_op jit(solution)/shard_map/all_gather | solution.py:76
  203.9 0.1 select_reduce_fusion.4
  204.0 0.7 copy.71
  204.7 0.7 copy.80
  205.4 3.1 %fusion.13 = (bf16[8,1,1,512,128]{4,3,2,1,0:T(8,128)(2,1)}, bf16[8,1,1,512,128]{4,3,2,1,0:T(8,128)(2,1)}) fusion(bf16[8,2,1,512,128]{4,3,2,1,0:T(8,128)(2,1)} %param.10), kind=kLoop, calls=%fused_computation.39 | loop fusion | bytes 4194304 | tf_op jit(solution)/shard_map/slice | solution.py:15
  208.5 2.7 %reshape.234 = bf16[8,1024,64]{2,1,0:T(8,128)(2,1)S(1)} reshape(bf16[8,1,1,512,128]{4,3,2,1,0:T(8,128)(2,1)} %get-tuple-element.15) | data formatting | bytes 2097152 | tf_op jit(solution)/shard_map/reshape.2
  211.2 0.1 fusion.7
  211.4 0.7 select_reduce_fusion.1
  212.1 0.1 copy.67
  212.2 0.7 copy.68
  212.9 0.2 convert_reduce_fusion
  213.1 0.1 copy.77
  213.2 0.7 copy.78
  213.9 2.7 %reshape.236 = bf16[8,1024,64]{2,1,0:T(8,128)(2,1)S(1)} reshape(bf16[8,1,1,512,128]{4,3,2,1,0:T(8,128)(2,1)} %get-tuple-element.16) | data formatting | bytes 2097152 | tf_op jit(solution)/shard_map/reshape.18
  216.6 1.3 multiply_add_fusion
  217.9 0.7 copy-done.1
  218.6 0.6 broadcast.96
  219.2 2.2 reduce.8
  221.4 1.1 reshape.264
  222.5 1.9 copy.74
  224.5 1.2 copy.75
  225.7 0.4 select_reduce_fusion
  226.1 1.1 fusion.3
  227.2 0.1 convert_element_type.60
  227.3 0.9 fusion.15
  228.2 34.4 %reduce-scatter.2.cloned.1.call-done = f32[8,256]{1,0:T(8,128)} async-done(((f32[8,2048]{1,0:T(8,128)}), f32[8,256]{1,0:T(8,128)}) %reduce-scatter.2.cloned.1.call-update) | async-done | bytes 8208 | tf_op jit(solution)/shard_map/reduce_scatter | solution.py:94
  262.6 1.3 convert_element_type.61
  (31 shorter events, 0.5 us)
Async XLA Ops:
  6.5 220.8 %copy-start = (bf16[256,2048]{1,0:T(8,128)(2,1)S(1)}, bf16[256,2048]{1,0:T(8,128)(2,1)}, u32[]{:S(2)}) copy-start(bf16[256,2048]{1,0:T(8,128)(2,1)} %param.15) | copy-start | bytes 3145732
  95.8 10.5 %copy-start.6 = (s32[8]{0:T(128)S(1)}, s32[8]{0:T(128)}, u32[]{:S(2)}) copy-start(s32[8]{0:T(128)} %param.13) | copy-start | bytes 100
  95.8 10.6 %copy-start.4 = (bf16[8,256]{1,0:T(8,128)(2,1)S(1)}, bf16[8,256]{1,0:T(8,128)(2,1)}, u32[]{:S(2)}) copy-start(bf16[8,256]{1,0:T(8,128)(2,1)} %param.8) | copy-start | bytes 12292
  95.8 10.8 %copy-start.5 = (bf16[8,2,64]{2,1,0:T(2,128)(2,1)S(1)}, bf16[8,2,64]{2,1,0:T(2,128)(2,1)}, u32[]{:S(2)}) copy-start(bf16[8,2,64]{2,1,0:T(2,128)(2,1)} %param.9) | copy-start | bytes 6148
  97.9 120.1 %all-to-all-start = ((f32[64,1,1024]{2,1,0:T(1,128)}), f32[64,1,1024]{2,1,0:T(1,128)S(1)}, u32[]{:S(2)}, u32[]{:S(2)}) async-start(f32[64,1,1024]{2,1,0:T(1,128)} %reshape.263), calls=%async_computation | async-start | bytes 524288 | tf_op jit(solution)/shard_map/all_to_all | solution.py:53
  106.2 156.4 %reduce-scatter.2.cloned.1.call-start = ((), (), s32[]{:S(2)}) async-start(), calls=%async_computation.2 | async-start | bytes 73728 | tf_op jit(solution)/shard_map/reduce_scatter | solution.py:94
  203.9 4.6 %copy-start.2 = (pred[8,256]{1,0:T(8,128)(4,1)}, pred[8,256]{1,0:T(8,128)(4,1)S(1)}, u32[]{:S(2)}) copy-start(pred[8,256]{1,0:T(8,128)(4,1)S(1)} %broadcast_compare_fusion) | copy-start | bytes 6148
  216.6 9.1 %copy-start.3 = (pred[8,256]{1,0:T(8,128)(4,1)S(1)}, pred[8,256]{1,0:T(8,128)(4,1)}, u32[]{:S(2)}) copy-start(pred[8,256]{1,0:T(8,128)(4,1)} %copy-done.2) | copy-start | bytes 6148
  217.9 0.7 copy-start.1
Sparse Core Ops, SparseCore 0:
  228.3 34.2 reduce-scatter.1
